TPU v7x, 128 devices: a whole 4x4x4 slice. The times are simulated.
128 devices in a mesh: row: 8 (over y_lo, z), col: 16 (over y_hi, x, core).
Axes of the slice: x: 4, y: 4 (y_hi: 2, y_lo: 2; y = y_hi * 2 + y_lo), z: 4, core: 2. Of those that a mesh axis runs over, the one named last changes fastest.
Arguments:
- features: bfloat16 [24576, 512], P(('col', 'row')), may hold values from -6 to 6
- out_grad: bfloat16 [24576, 512], P(('row', 'col')), may hold values from -6 to 6
- weight: bfloat16 [512, 512], replicated, may hold values from -0.25 to 0.25
- block_values: bfloat16 [8, 16, 288, 4096], P('row', 'col'), may hold values from -0.125 to 0.125
- block_coords: int32 [8, 16, 2, 288], P('row', 'col'), may hold values from 0 to 47, as said below
- block_counts: int32 [8, 16], P('row', 'col'), may hold values from 1 to 288, as said below
Outputs:
- activations: bfloat16 [24576, 512], P(('row', 'col'))
- weight_grad: float32 [512, 512], replicated
- feature_grad: bfloat16 [24576, 512], P(('col', 'row'))
Inputs may be any that keep to these rules, and one draw needn't show every extreme that they name: `block_coords`: entry 0 of a slot is a block row below 48, entry 1 a block column below 24; the 288 slots of a tile name distinct blocks. `block_counts`: slots from the count onward are padding: their coordinates and values are ignored. Some tile has exactly 288 live slots.
All inputs are finite; a program needn't handle non-finite values.
Results may differ from a plain program's by a relative error of at most 0.025.
Values may be sent and summed in bfloat16 or wider, within the bound.
No kernel may reach another device: no remote copies, remote signals or barrier semaphores. Data moves between devices by JAX's collectives and lax.ppermute only.
A program may use at most 128 MiB of HBM per device.

v0:
```python
import math
import jax
import jax.numpy as jnp
from jax import lax
from jax.sharding import PartitionSpec as P


def settle(term):
    return lax.optimization_barrier(term.astype(jnp.bfloat16)).astype(jnp.float32)


def per_device(features, out_grad, weight, block_values, block_coords, block_counts):
    row_devices = lax.axis_size("row")
    col_devices = lax.axis_size("col")
    node_count = features.shape[0]
    side = 64
    slot_total = block_values.shape[2]
    block_rows = node_count * col_devices // side
    block_cols = node_count * row_devices // side
    live_count = block_counts[0, 0]
    row_ids = block_coords[0, 0, 0]
    col_ids = block_coords[0, 0, 1]
    slot_vals = block_values.reshape(slot_total, side, side)
    live = jnp.arange(slot_total, dtype=jnp.int32) < live_count
    slot_vals = jnp.where(live[:, None, None], slot_vals, jnp.zeros_like(slot_vals))
    panel = lax.all_gather(features, "row", axis=0, tiled=True)
    dense_tile = jnp.zeros((block_rows, side, block_cols, side), jnp.bfloat16)
    dense_tile = dense_tile.at[row_ids, :, col_ids, :].add(slot_vals)
    dense_tile = dense_tile.reshape(block_rows * side, block_cols * side)
    partial_agg = settle(jnp.dot(dense_tile, panel, preferred_element_type=jnp.float32))
    aggregated = lax.psum_scatter(
        partial_agg.astype(jnp.bfloat16), "col", scatter_dimension=0, tiled=True
    )
    pre_act = jnp.dot(aggregated, weight, preferred_element_type=jnp.float32)
    sigmoid_pre = jax.nn.sigmoid(pre_act)
    activations = (pre_act * sigmoid_pre).astype(jnp.bfloat16)
    grad_pre = (
        out_grad.astype(jnp.float32) * sigmoid_pre * (1.0 + pre_act * (1.0 - sigmoid_pre))
    ).astype(jnp.bfloat16)
    activations, grad_pre = (activations, grad_pre)
    grad_agg = lax.dot_general(
        grad_pre, weight, (((1,), (1,)), ((), ())), preferred_element_type=jnp.float32
    ).astype(jnp.bfloat16)
    grad_rows = lax.all_gather(grad_agg, "col", axis=0, tiled=True)
    local_wgrad = lax.dot_general(
        aggregated, grad_pre, (((0,), (0,)), ((), ())), preferred_element_type=jnp.float32
    )
    total_nodes = node_count * row_devices * col_devices
    weight_grad = lax.psum(local_wgrad, ("row", "col")) * jnp.float32(1.0 / math.sqrt(total_nodes))
    partial_grad = settle(
        lax.dot_general(
            dense_tile, grad_rows, (((0,), (0,)), ((), ())), preferred_element_type=jnp.float32
        )
    )
    feature_grad = lax.psum_scatter(
        partial_grad.astype(jnp.bfloat16), "row", scatter_dimension=0, tiled=True
    )
    return (activations, weight_grad, feature_grad)


def solution(mesh):
    return jax.shard_map(
        per_device,
        mesh=mesh,
        in_specs=(
            P(("col", "row"), None),
            P(("row", "col"), None),
            P(),
            P("row", "col", None, None),
            P("row", "col", None, None),
            P("row", "col"),
        ),
        out_specs=(P(("row", "col"), None), P(), P(("col", "row"), None)),
        check_vma=False,
    )
```

profile of v0, /device:TPU:0, one launch (start us, length us, event | category | flops | bytes accessed | tf_op | source)
XLA Modules:
  0.0 468.9 jit_solution(1539356239016432633)
XLA Ops:
  7.2 0.0 all-gather.3.cloned.1.call-start
  7.2 0.7 all-gather.3.cloned.1.call-update
  7.9 0.0 reduce-scatter.3.cloned.1.call-start
  8.0 4.5 copy.9
  13.1 3.9 broadcast_select_fusion
  17.0 9.9 %copy.10 = bf16[288,64,64]{2,1,0:T(8,128)(2,1)} copy(bf16[288,64,64]{0,2,1:T(8,128)(2,1)} %broadcast_select_fusion) | data formatting | bytes 4718592 | tf_op jit(solution)/shard_map/jit(_where)/select_n | solution.py:25
  26.9 7.1 %broadcast_in_dim.17 = bf16[48,64,24,64]{3,1,2,0:T(8,128)(2,1)} broadcast(bf16[]{:T(256)} %constant.6.clone.1), dimensions={} | broadcast | bytes 9437186 | tf_op jit(solution)/shard_map/broadcast_in_dim | solution.py:27
  34.0 45.5 %scatter_fusion = bf16[48,64,24,64]{3,1,2,0:T(8,128)(2,1)} fusion(bf16[48,64,24,64]{3,1,2,0:T(8,128)(2,1)} %broadcast_in_dim.17, s32[288]{0:T(512)S(1)} %fusion.1, bf16[288,64,64]{2,1,0:T(8,128)(2,1)} %copy.10), kind=kCustom, calls=%fused_computation | custom fusion | flops 1179648 | bytes 7080192 | tf_op jit(solution)/shard_map/scatter-add | solution.py:28
  79.6 22.7 %copy.11 = bf16[48,64,24,64]{3,2,1,0:T(8,128)(2,1)} copy(bf16[48,64,24,64]{3,1,2,0:T(8,128)(2,1)} %scatter_fusion) | data formatting | bytes 18874368 | tf_op jit(solution)/shard_map/scatter-add | solution.py:28
  102.2 24.6 %reshape.73 = bf16[3072,1536]{1,0:T(8,128)(2,1)} reshape(bf16[48,64,24,64]{3,2,1,0:T(8,128)(2,1)} %copy.11) | data formatting | bytes 18874368 | tf_op jit(solution)/shard_map/reshape | solution.py:29
  126.8 9.2 %convolution_convert_fusion = bf16[3072,512]{1,0:T(8,128)(2,1)} fusion(bf16[3072,1536]{1,0:T(8,128)(2,1)} %reshape.73, bf16[1536,512]{1,0:T(8,128)(2,1)} %all-gather.3.cloned.1.call-done), kind=kOutput, calls=%fused_computation.1 | convolution fusion | flops 4833411072 | bytes 14155776 | tf_op jit(solution)/shard_map/dot_general | solution.py:30
  136.1 0.0 reduce-scatter.3.cloned.1.call-update
  136.1 0.0 all-gather.5.cloned.1.call-start
  136.1 77.8 %reduce-scatter.3.cloned.1.call-done = bf16[192,512]{1,0:T(8,128)(2,1)} async-done(((bf16[3072,512]{1,0:T(8,128)(2,1)}), bf16[192,512]{1,0:T(8,128)(2,1)}) %reduce-scatter.3.cloned.1.call-update) | async-done | bytes 196624 | tf_op jit(solution)/shard_map/reduce_scatter | solution.py:31
  213.9 2.0 multiply_convert_fusion.1
  216.0 1.0 convolution_convert_fusion.2
  217.0 0.0 all-reduce.2.cloned.1.call-start
  217.1 1.4 fusion.2
  218.5 0.2 reduce-scatter.5.cloned.1.call-start
  218.7 49.6 %all-gather.5.cloned.1.call-done = bf16[3072,512]{1,0:T(8,128)(2,1)} async-done(((bf16[192,512]{1,0:T(8,128)(2,1)}), bf16[3072,512]{1,0:T(8,128)(2,1)}) %all-gather.5.cloned.1.call-update) | async-done | bytes 3145744 | tf_op jit(solution)/shard_map/all_gather | solution.py:44
  268.3 10.4 %convolution_convert_fusion.1 = bf16[1536,512]{1,0:T(8,128)(2,1)} fusion(bf16[3072,1536]{1,0:T(8,128)(2,1)} %reshape.73, bf16[3072,512]{1,0:T(8,128)(2,1)} %all-gather.5.cloned.1.call-done), kind=kOutput, calls=%fused_computation.3 | convolution fusion | flops 4832624640 | bytes 14155776 | tf_op jit(solution)/shard_map/dot_general | solution.py:51
  278.7 140.3 %all-reduce.2.cloned.1.call-done = f32[512,512]{1,0:T(8,128)} async-done(((f32[512,512]{1,0:T(8,128)}), f32[512,512]{1,0:T(8,128)}) %all-reduce.2.cloned.1.call-update) | async-done | bytes 1048592 | tf_op jit(solution)/shard_map/psum | solution.py:49
  419.0 2.3 broadcast_multiply_fusion
  421.3 41.0 %reduce-scatter.5.cloned.1.call-done = bf16[192,512]{1,0:T(8,128)(2,1)} async-done(((bf16[1536,512]{1,0:T(8,128)(2,1)}), bf16[192,512]{1,0:T(8,128)(2,1)}) %reduce-scatter.5.cloned.1.call-update) | async-done | bytes 196624 | tf_op jit(solution)/shard_map/reduce_scatter | solution.py:55
  (14 shorter events, 0.1 us)
Async XLA Ops:
  7.2 206.8 %copy-start = (bf16[512,512]{1,0:T(8,128)(2,1)S(1)}, bf16[512,512]{1,0:T(8,128)(2,1)}, u32[]{:S(2)}) copy-start(bf16[512,512]{1,0:T(8,128)(2,1)} %param.8) | copy-start | bytes 1572868
  7.2 119.6 %all-gather.3.cloned.1.call-start = ((), (), s32[]{:S(2)}) async-start(), calls=%async_computation.2 | async-start | bytes 1769472 | tf_op jit(solution)/shard_map/all_gather | solution.py:26
  7.9 206.0 %reduce-scatter.3.cloned.1.call-start = ((), (), s32[]{:S(2)}) async-start(), calls=%async_computation.3 | async-start | bytes 3342336 | tf_op jit(solution)/shard_map/reduce_scatter | solution.py:31
  17.0 10.0 %copy-start.1 = (s32[1,1,2,288]{3,2,1,0:T(2,128)S(1)}, s32[1,1,2,288]{3,2,1,0:T(2,128)}, u32[]{:S(2)}) copy-start(s32[1,1,2,288]{3,2,1,0:T(2,128)} %param.10) | copy-start | bytes 6916
  136.1 79.9 %copy-start.2 = (bf16[192,512]{1,0:T(8,128)(2,1)S(1)}, bf16[192,512]{1,0:T(8,128)(2,1)}, u32[]{:S(2)}) copy-start(bf16[192,512]{1,0:T(8,128)(2,1)} %param.7) | copy-start | bytes 589828
  136.1 132.2 %all-gather.5.cloned.1.call-start = ((), (), s32[]{:S(2)}) async-start(), calls=%async_computation.5 | async-start | bytes 3342336 | tf_op jit(solution)/shard_map/all_gather | solution.py:44
  213.9 3.1 copy-start.3
  217.0 202.0 %all-reduce.2.cloned.1.call-start = ((), (), s32[]{:S(2)}) async-start(), calls=%async_computation.4 | async-start | bytes 2097152 | tf_op jit(solution)/shard_map/psum | solution.py:49
  218.5 243.9 %reduce-scatter.5.cloned.1.call-start = ((), (), s32[]{:S(2)}) async-start(), calls=%async_computation.6 | async-start | bytes 1769472 | tf_op jit(solution)/shard_map/reduce_scatter | solution.py:55
Sparse Core Ops, SparseCore 0:
  9.7 43.1 all-gather.2
  136.2 77.6 reduce-scatter.2
  217.1 51.1 all-gather.4
  273.5 145.4 all-reduce.1
  422.0 40.3 reduce-scatter.4
where the time goes:
time: 471 us; the launch traced here: 469 us
  waiting for transfers between devices  309 us (66%)
  local copies, waits for them, and re-layouts  68.8 us (15%)
  other arithmetic  51.7 us (11%)
  matrix products  24.1 us (5%)
  between operations  14.5 us (3%)
    psum x1, waiting for transfers between devices, per_device(): lax.psum(local_wgrad, ('row', 'col'))  140 us
    reduce_scatter x1, waiting for transfers between devices, per_device(): lax.psum_scatter(partial_agg.astype(jnp.bfloat16), 'col', scatter_dimensi...  77.8 us
    all_gather x1, waiting for transfers between devices, per_device(): grad_rows = lax.all_gather(grad_agg, 'col', axis=0, tiled=True)  49.6 us
    scatter-add x1, other arithmetic, per_device(): dense_tile = dense_tile.at[row_ids, :, col_ids, :].add(slot_vals)  45.5 us
    reduce_scatter x1, waiting for transfers between devices, per_device(): lax.psum_scatter(partial_grad.astype(jnp.bfloat16), 'row', scatter_dimens...  41 us
    reshape x1, local copies, waits for them, and re-layouts, per_device(): dense_tile = dense_tile.reshape(block_rows * side, block_cols * side)  24.6 us
    scatter-add x1, local copies, waits for them, and re-layouts, per_device(): dense_tile = dense_tile.at[row_ids, :, col_ids, :].add(slot_vals)  22.7 us
    dot_general x1, matrix products, per_device(): lax.dot_general(dense_tile, grad_rows, (((0,), (0,)), ((), ())), preferre...  10.4 us
  transfers between devices with their start and end apart: 5, of which 4 were waited for; matrix products, arithmetic and copies ran while one was open for 28% of the time, Pallas kernels for 0%

commit v1 on v0

--- a/solution.py
+++ b/solution.py
@@ -41,7 +41,9 @@
     grad_agg = lax.dot_general(
         grad_pre, weight, (((1,), (1,)), ((), ())), preferred_element_type=jnp.float32
     ).astype(jnp.bfloat16)
-    grad_rows = lax.all_gather(grad_agg, "col", axis=0, tiled=True)
+    grad_rows = jnp.concatenate(
+        lax.all_to_all(jnp.stack([grad_agg] * lax.axis_size("col")), "col", 0, 0), axis=0
+    )
     local_wgrad = lax.dot_general(
         aggregated, grad_pre, (((0,), (0,)), ((), ())), preferred_element_type=jnp.float32
     )

time: 471 us -> 444 us (0.943)
  waiting for transfers between devices: 309 us -> 277 us
    all_gather x1 -> x0, waiting for transfers between devices: 49.6 us -> none  [per_device(): grad_rows = lax.all_gather(grad_agg, 'col', axis=0, tiled=True)]
    all_to_all x0 -> x1, waiting for transfers between devices: none -> 40.9 us  [per_device(): lax.all_to_all(jnp.stack([grad_agg] * lax.axis_size('col')), 'col', 0, 0)]
    psum x1, waiting for transfers between devices: 140 us -> 116 us  [per_device(): lax.psum(local_wgrad, ('row', 'col'))]
  transfers between devices with their start and end apart: 5 -> 5, of which waited for: 4 -> 4; matrix products, arithmetic and copies ran while one was open for 28% -> 30% of each run, Pallas kernels for 0% -> 0%
where the time goes in v1:
time: 444 us; the launch traced here: 442 us
  waiting for transfers between devices  277 us (62%)
  local copies, waits for them, and re-layouts  70.7 us (16%)
  other arithmetic  51.7 us (12%)
  matrix products  23.4 us (5%)
  between operations  14.5 us (3%)
  starting transfers between devices  4.96 us (1%)
    psum x1, waiting for transfers between devices, per_device(): lax.psum(local_wgrad, ('row', 'col'))  116 us
    reduce_scatter x1, waiting for transfers between devices, per_device(): lax.psum_scatter(partial_agg.astype(jnp.bfloat16), 'col', scatter_dimensi...  77.9 us
    scatter-add x1, other arithmetic, per_device(): dense_tile = dense_tile.at[row_ids, :, col_ids, :].add(slot_vals)  45.6 us
    reduce_scatter x1, waiting for transfers between devices, per_device(): lax.psum_scatter(partial_grad.astype(jnp.bfloat16), 'row', scatter_dimens...  41 us
    all_to_all x1, waiting for transfers between devices, per_device(): lax.all_to_all(jnp.stack([grad_agg] * lax.axis_size('col')), 'col', 0, 0)  40.9 us
    reshape x1, local copies, waits for them, and re-layouts, per_device(): dense_tile = dense_tile.reshape(block_rows * side, block_cols * side)  24.6 us
    scatter-add x1, local copies, waits for them, and re-layouts, per_device(): dense_tile = dense_tile.at[row_ids, :, col_ids, :].add(slot_vals)  22.7 us
    dot_general x1, matrix products, per_device(): lax.dot_general(dense_tile, grad_rows, (((0,), (0,)), ((), ())), preferre...  10.5 us
  transfers between devices with their start and end apart: 5, of which 4 were waited for; matrix products, arithmetic and copies ran while one was open for 30% of the time, Pallas kernels for 0%

profile of v1, /device:TPU:0, one launch (start us, length us, event | category | flops | bytes accessed | tf_op | source)
XLA Modules:
  0.0 441.9 jit_solution(3526511494331733221)
XLA Ops:
  7.2 0.0 all-gather.2.cloned.1.call-start
  7.2 0.7 all-gather.2.cloned.1.call-update
  7.9 0.0 reduce-scatter.3.cloned.1.call-start
  8.0 4.5 %copy.9 = bf16[1,1,288,4096]{2,3,1,0:T(8,128)(2,1)} copy(bf16[1,1,288,4096]{3,2,1,0:T(8,128)(2,1)} %param.9) | data formatting | bytes 4718592 | tf_op args[3]
  13.1 3.8 broadcast_select_fusion
  17.0 9.9 %copy.10 = bf16[288,64,64]{2,1,0:T(8,128)(2,1)} copy(bf16[288,64,64]{0,2,1:T(8,128)(2,1)} %broadcast_select_fusion) | data formatting | bytes 4718592 | tf_op jit(solution)/shard_map/jit(_where)/select_n | solution.py:25
  26.9 7.0 %broadcast_in_dim.17 = bf16[48,64,24,64]{3,1,2,0:T(8,128)(2,1)} broadcast(bf16[]{:T(256)} %constant.6.clone.1), dimensions={} | broadcast | bytes 9437186 | tf_op jit(solution)/shard_map/broadcast_in_dim | solution.py:27
  33.9 45.6 %scatter_fusion = bf16[48,64,24,64]{3,1,2,0:T(8,128)(2,1)} fusion(bf16[48,64,24,64]{3,1,2,0:T(8,128)(2,1)} %broadcast_in_dim.17, s32[288]{0:T(512)S(1)} %fusion.1, bf16[288,64,64]{2,1,0:T(8,128)(2,1)} %copy.10), kind=kCustom, calls=%fused_computation | custom fusion | flops 1179648 | bytes 7080192 | tf_op jit(solution)/shard_map/scatter-add | solution.py:28
  79.5 22.7 %copy.11 = bf16[48,64,24,64]{3,2,1,0:T(8,128)(2,1)} copy(bf16[48,64,24,64]{3,1,2,0:T(8,128)(2,1)} %scatter_fusion) | data formatting | bytes 18874368 | tf_op jit(solution)/shard_map/scatter-add | solution.py:28
  102.2 24.6 %reshape.78 = bf16[3072,1536]{1,0:T(8,128)(2,1)} reshape(bf16[48,64,24,64]{3,2,1,0:T(8,128)(2,1)} %copy.11) | data formatting | bytes 18874368 | tf_op jit(solution)/shard_map/reshape | solution.py:29
  126.8 9.2 %convolution_convert_fusion = bf16[3072,512]{1,0:T(8,128)(2,1)} fusion(bf16[3072,1536]{1,0:T(8,128)(2,1)} %reshape.78, bf16[1536,512]{1,0:T(8,128)(2,1)} %all-gather.2.cloned.1.call-done), kind=kOutput, calls=%fused_computation.1 | convolution fusion | flops 4833411072 | bytes 14155776 | tf_op jit(solution)/shard_map/dot_general | solution.py:30
  136.1 77.9 %reduce-scatter.3.cloned.1.call-done = bf16[192,512]{1,0:T(8,128)(2,1)} async-done(((bf16[3072,512]{1,0:T(8,128)(2,1)}), bf16[192,512]{1,0:T(8,128)(2,1)}) %reduce-scatter.3.cloned.1.call-update) | async-done | bytes 196624 | tf_op jit(solution)/shard_map/reduce_scatter | solution.py:31
  213.9 1.9 multiply_convert_fusion.1
  215.9 0.3 convolution_convert_fusion.2
  216.2 2.0 stack.2
  218.2 4.6 %all-to-all-start = ((bf16[16,192,512]{2,1,0:T(8,128)(2,1)}), bf16[16,192,512]{2,1,0:T(8,128)(2,1)}, u32[]{:S(2)}, u32[]{:S(2)}) async-start(bf16[16,192,512]{2,1,0:T(8,128)(2,1)} %stack.2), calls=%async_computation.1 | async-start | bytes 6291456 | tf_op jit(solution)/shard_map/all_to_all | solution.py:45
  222.8 0.0 all-reduce.2.cloned.1.call-start
  222.8 1.4 fusion.2
  224.3 0.2 reduce-scatter.5.cloned.1.call-start
  224.5 40.9 %all-to-all-done = bf16[16,192,512]{2,1,0:T(8,128)(2,1)} async-done(((bf16[16,192,512]{2,1,0:T(8,128)(2,1)}), bf16[16,192,512]{2,1,0:T(8,128)(2,1)}, u32[]{:S(2)}, u32[]{:S(2)}) %all-to-all-start) | async-done | bytes 3145760 | tf_op jit(solution)/shard_map/all_to_all | solution.py:45
  265.4 10.5 %convolution_convert_fusion.1 = bf16[1536,512]{1,0:T(8,128)(2,1)} fusion(bf16[3072,1536]{1,0:T(8,128)(2,1)} %reshape.78, bf16[3072,512]{1,0:T(8,128)(2,1)} %bitcast.4), kind=kOutput, calls=%fused_computation.3 | convolution fusion | flops 4832624640 | bytes 14155776 | tf_op jit(solution)/shard_map/dot_general | solution.py:53
  275.8 116.2 %all-reduce.2.cloned.1.call-done = f32[512,512]{1,0:T(8,128)} async-done(((f32[512,512]{1,0:T(8,128)}), f32[512,512]{1,0:T(8,128)}) %all-reduce.2.cloned.1.call-update) | async-done | bytes 1048592 | tf_op jit(solution)/shard_map/psum | solution.py:51
  392.1 2.3 broadcast_multiply_fusion
  394.4 41.0 %reduce-scatter.5.cloned.1.call-done = bf16[192,512]{1,0:T(8,128)(2,1)} async-done(((bf16[1536,512]{1,0:T(8,128)(2,1)}), bf16[192,512]{1,0:T(8,128)(2,1)}) %reduce-scatter.5.cloned.1.call-update) | async-done | bytes 196624 | tf_op jit(solution)/shard_map/reduce_scatter | solution.py:57
  (14 shorter events, 0.1 us)
Async XLA Ops:
  7.2 206.8 %copy-start = (bf16[512,512]{1,0:T(8,128)(2,1)S(1)}, bf16[512,512]{1,0:T(8,128)(2,1)}, u32[]{:S(2)}) copy-start(bf16[512,512]{1,0:T(8,128)(2,1)} %param.8) | copy-start | bytes 1572868
  7.2 119.6 %all-gather.2.cloned.1.call-start = ((), (), s32[]{:S(2)}) async-start(), calls=%async_computation.3 | async-start | bytes 1769472 | tf_op jit(solution)/shard_map/all_gather | solution.py:26
  7.9 206.0 %reduce-scatter.3.cloned.1.call-start = ((), (), s32[]{:S(2)}) async-start(), calls=%async_computation.4 | async-start | bytes 3342336 | tf_op jit(solution)/shard_map/reduce_scatter | solution.py:31
  17.0 9.9 %copy-start.1 = (s32[1,1,2,288]{3,2,1,0:T(2,128)S(1)}, s32[1,1,2,288]{3,2,1,0:T(2,128)}, u32[]{:S(2)}) copy-start(s32[1,1,2,288]{3,2,1,0:T(2,128)} %param.10) | copy-start | bytes 6916
  136.0 79.8 %copy-start.2 = (bf16[192,512]{1,0:T(8,128)(2,1)S(1)}, bf16[192,512]{1,0:T(8,128)(2,1)}, u32[]{:S(2)}) copy-start(bf16[192,512]{1,0:T(8,128)(2,1)} %param.7) | copy-start | bytes 589828
  218.2 4.7 %copy-start.3 = (bf16[192,512]{1,0:T(8,128)(2,1)S(1)}, bf16[192,512]{1,0:T(8,128)(2,1)}, u32[]{:S(2)}) copy-start(bf16[192,512]{1,0:T(8,128)(2,1)} %reduce-scatter.3.cloned.1.call-done) | copy-start | bytes 589828
  218.2 47.2 %all-to-all-start = ((bf16[16,192,512]{2,1,0:T(8,128)(2,1)}), bf16[16,192,512]{2,1,0:T(8,128)(2,1)}, u32[]{:S(2)}, u32[]{:S(2)}) async-start(bf16[16,192,512]{2,1,0:T(8,128)(2,1)} %stack.2), calls=%async_computation.1 | async-start | bytes 6291456 | tf_op jit(solution)/shard_map/all_to_all | solution.py:45
  222.8 169.3 %all-reduce.2.cloned.1.call-start = ((), (), s32[]{:S(2)}) async-start(), calls=%async_computation.5 | async-start | bytes 2097152 | tf_op jit(solution)/shard_map/psum | solution.py:51
  224.3 211.1 %reduce-scatter.5.cloned.1.call-start = ((), (), s32[]{:S(2)}) async-start(), calls=%async_computation.6 | async-start | bytes 1769472 | tf_op jit(solution)/shard_map/reduce_scatter | solution.py:57
Sparse Core Ops, SparseCore 0:
  9.7 43.1 all-gather.1
  136.2 77.6 reduce-scatter.2
  229.0 163.0 all-reduce.1
  395.0 40.3 reduce-scatter.4
